TPU v7x, 128 devices: a whole 4x4x4 slice. The times are simulated.
128 devices in a mesh: el: 8 (over x, core), tg: 16 (over y, z).
Axes of the slice: x: 4, y: 4, z: 4, core: 2. Of those that a mesh axis runs over, the one named last changes fastest.
Arguments:
- field_points: bfloat16 [65536, 16, 256], P(('el', 'tg')), may hold values from -6 to 6
- owner_map: int32 [128, 512], P(('el', 'tg')), may hold values from 0 to 127, as said below
- send_counts: int32 [128, 512], P(('el', 'tg')), may hold values from 15 to 16
- tile_rows: int32 [128, 32], P(('el', 'tg')), may hold values from 0 to 31, each once within a row
- tile_cols: int32 [128, 32, 16], P(('el', 'tg')), may hold values from 0 to 63, as said below
- weights: bfloat16 [128, 32, 16, 128, 128], P(('el', 'tg')), may hold values from -0.125 to 0.125
Outputs:
- remapped: bfloat16 [256, 524288], P('el', 'tg')
Inputs may be any that keep to these rules, and one draw needn't show every extreme that they name: `owner_map`: each device's 512 elements name every owner exactly 4 times. `tile_cols`: the 16 entries of one target tile are distinct.
All inputs are finite; a program needn't handle non-finite values.
Results may differ from a plain program's by a relative error of at most 0.001.
Values may be sent and summed in bfloat16 or wider, within the bound.
No kernel may reach another device: no remote copies, remote signals or barrier semaphores. Data moves between devices by JAX's collectives and lax.ppermute only.
A program may use at most 128 MiB of HBM per device.

v0:
```python
import functools

import jax
import jax.numpy as jnp
from jax import lax
from jax.experimental import pallas as pl
from jax.experimental.pallas import tpu as pltpu
from jax.sharding import PartitionSpec as P

SHARES = (7, 9)
STAGED = 6
CHIPS = (2, 1, 3, 0)
GROUP = 4
AHEAD = 2
HOPS = ((2, 0), (2, 1), (1, 0), (3, 0), (1, 1), (3, 1), (0, 1), (0, 0))


def pack_kernel(chunks, owner_ref, counts_ref, field_ref, out_ref, buf, dst, pos_v, pos_s, sem_in, sem_pos, sem_out):
    elems, points, channels = dst.shape
    step = elems // chunks
    owners = elems // 4
    def fetch(c):
        return pltpu.make_async_copy(field_ref.at[pl.ds(c * step, step)], buf.at[pl.ds(c * step, step)], sem_in.at[c])
    for c in range(chunks):
        fetch(c).start()
    owner = owner_ref[...]
    hit = lax.broadcasted_iota(jnp.int32, (owners, elems), 0) == owner
    hit = jnp.where(hit, 1.0, 0.0)
    before = jnp.where(lax.broadcasted_iota(jnp.int32, (elems, elems), 0) < lax.broadcasted_iota(jnp.int32, (elems, elems), 1), 1.0, 0.0)
    earlier = jnp.dot(hit.astype(jnp.bfloat16), before.astype(jnp.bfloat16), preferred_element_type=jnp.float32)
    rank = jnp.sum(hit * earlier, axis=0, keepdims=True)
    pos_v[...] = owner * 4 + rank.astype(jnp.int32)
    cp = pltpu.make_async_copy(pos_v, pos_s, sem_pos)
    cp.start()
    cp.wait()
    point = lax.broadcasted_iota(jnp.int32, (points, channels), 0)
    for c in range(chunks):
        fetch(c).wait()
        def body(e, carry):
            live = point < counts_ref[0, e]
            dst[pos_s[0, e]] = jnp.where(live, buf[e], jnp.zeros((), buf.dtype))
            return carry
        lax.fori_loop(c * step, (c + 1) * step, body, 0, unroll=8)
    out = pltpu.make_async_copy(dst, out_ref, sem_out)
    out.start()
    out.wait()


def pack(owner_map, send_counts, field, chunks=8):
    return pl.pallas_call(
        functools.partial(pack_kernel, chunks),
        out_shape=jax.ShapeDtypeStruct(field.shape, field.dtype),
        in_specs=[pl.BlockSpec(memory_space=pltpu.VMEM), pl.BlockSpec(memory_space=pltpu.SMEM), pl.BlockSpec(memory_space=pl.ANY)],
        out_specs=pl.BlockSpec(memory_space=pl.ANY),
        scratch_shapes=[
            pltpu.VMEM(field.shape, field.dtype),
            pltpu.VMEM(field.shape, field.dtype),
            pltpu.VMEM((1, field.shape[0]), jnp.int32),
            pltpu.SMEM((1, field.shape[0]), jnp.int32),
            pltpu.SemaphoreType.DMA((chunks,)),
            pltpu.SemaphoreType.DMA,
            pltpu.SemaphoreType.DMA,
        ],
        name="pack",
    )(owner_map, send_counts, field)


HOPS_OF = {False: HOPS, True: tuple((chip, 0) for chip in CHIPS)}


def peer(me, groups, hop):
    chip, core = me // 2, me % 2
    return lax.rem(chip + hop[0], groups // 2) * 2 + (1 - core if hop[1] else core)


def stage_kernel(rows_ref, w_ref, out_ref, order, sems):
    for t in range(rows_ref.shape[1]):
        order[rows_ref[0, t]] = t
    copies = [pltpu.make_async_copy(w_ref.at[0, order[q]], out_ref.at[q], sems.at[q]) for q in range(STAGED)]
    for copy in copies:
        copy.start()
    for copy in copies:
        copy.wait()


def stage(tile_rows, weights):
    return pl.pallas_call(
        stage_kernel,
        out_shape=jax.ShapeDtypeStruct((STAGED, *weights.shape[2:]), weights.dtype),
        in_specs=[pl.BlockSpec(memory_space=pltpu.SMEM), pl.BlockSpec(memory_space=pl.ANY)],
        out_specs=pl.BlockSpec(memory_space=pltpu.VMEM),
        scratch_shapes=[pltpu.SMEM(tile_rows.shape[1:], jnp.int32), pltpu.SemaphoreType.DMA((STAGED,))],
        compiler_params=pltpu.CompilerParams(vmem_limit_bytes=46 << 20),
        cost_estimate=pl.CostEstimate(flops=0, bytes_accessed=4 * STAGED * weights[0, 0].size, transcendentals=0),
        name="stage",
    )(tile_rows, weights)


def remap_kernel(first, staged, paired, axis, rows_ref, cols_ref, w_ref, src_ref, *refs):
    outs, (w_buf, out, order, sem_src, sem_w) = list(refs[staged > 0 : -5]), refs[-5:]
    src = src_ref
    _, targets, blocks, tile, _ = w_ref.shape
    count = out.shape[1] // tile
    groups = len(HOPS)
    rows = out.shape[0] // groups
    if staged:
        src = outs.pop()
        load = pltpu.make_async_copy(src_ref, src, sem_src)
        load.start()
    for t in range(targets):
        order[rows_ref[0, t]] = t

    def fetch(q):
        return pltpu.make_async_copy(w_ref.at[0, order[first + q]], w_buf.at[q - staged], sem_w.at[q - staged])

    def block(q, k):
        return refs[0][q, k] if q < staged else w_buf[q - staged, k]

    for q in range(staged, GROUP * AHEAD):
        fetch(q).start()
    if staged:
        load.wait()
    for g in range(0, count, GROUP):
        for q in range(max(g, staged), min(count, g + GROUP)):
            fetch(q).wait()
        for q in range(g + GROUP * AHEAD, min(count, g + GROUP * AHEAD + GROUP)):
            fetch(q).start()
        for q in range(g, min(count, g + GROUP)):
            t = order[first + q]
            total = None
            for k in range(0, blocks, 2):
                w = jnp.concatenate([block(q, k), block(q, k + 1)], axis=1)
                x = jnp.concatenate([src[cols_ref[0, t, k]], src[cols_ref[0, t, k + 1]]], axis=0)
                r = jnp.dot(w, x, preferred_element_type=jnp.float32)
                total = r if total is None else total + r
            out[:, q * tile : (q + 1) * tile] = total.T.astype(out.dtype)
    me = lax.axis_index(axis) if axis else 0
    for piece, hop in zip(outs, HOPS_OF[paired]):
        row = peer(me, groups, hop) // 2 * 2 if paired else peer(me, groups, hop)
        piece[...] = out[pl.ds(pl.multiple_of(row * rows, rows), piece.shape[0])]


def remap(first, count, paired, tile_rows, tile_cols, weights, source, ready=None, axis="el"):
    _, targets, blocks, tile, _ = weights.shape
    channels = source.shape[-1]
    staged = 0 if ready is None else STAGED
    pieces = len(HOPS_OF[paired])
    shapes = [jax.ShapeDtypeStruct((channels // pieces, count * tile), source.dtype)] * pieces
    vmem = pl.BlockSpec(memory_space=pltpu.VMEM)
    held = [pl.BlockSpec(memory_space=pl.ANY), vmem] if staged else [vmem]
    if staged:
        shapes.append(jax.ShapeDtypeStruct(source.shape, source.dtype))
    return pl.pallas_call(
        functools.partial(remap_kernel, first, staged, paired, axis),
        out_shape=shapes,
        in_specs=[pl.BlockSpec(memory_space=pltpu.SMEM)] * 2 + [pl.BlockSpec(memory_space=pl.ANY)] + held,
        out_specs=[vmem] * len(shapes),
        scratch_shapes=[
            pltpu.VMEM((count - staged, *weights.shape[2:]), weights.dtype),
            pltpu.VMEM((channels, count * tile), source.dtype),
            pltpu.SMEM((targets,), jnp.int32),
            pltpu.SemaphoreType.DMA,
            pltpu.SemaphoreType.DMA((count - staged,)),
        ],
        compiler_params=pltpu.CompilerParams(vmem_limit_bytes=46 << 20),
        cost_estimate=pl.CostEstimate(
            flops=2 * count * blocks * tile * tile * channels,
            bytes_accessed=2 * (weights.size * count // targets + source.size),
            transcendentals=0,
        ),
    )(tile_rows, tile_cols, weights, source, *([ready] if staged else []))


def place(me, groups, start, piece, hop, out_ref, sem):
    chip, core = hop
    source = peer(me, groups, ((groups // 2 - chip) % (groups // 2), core))
    lane = pl.multiple_of(source * (out_ref.shape[1] // groups) + start, 128)
    return pltpu.make_async_copy(piece, out_ref.at[:, pl.ds(lane, piece.shape[1])], sem)


def join_kernel(start, groups, hops, axis, *refs):
    out_ref, sems = refs[-2:]
    me = lax.axis_index(axis) if axis else 0
    rows = out_ref.shape[0]
    stores = []
    for i, hop in enumerate(hops):
        piece = refs[i] if len(hops) == groups else refs[0].at[pl.ds(i * rows, rows)]
        stores.append(place(me, groups, start, piece, hop, out_ref, sems.at[i]))
        stores[i].start()
    for store in stores:
        store.wait()


def join(start, hops, groups, pieces, whole, axis="el"):
    return pl.pallas_call(
        functools.partial(join_kernel, start, groups, hops, axis),
        out_shape=jax.ShapeDtypeStruct(whole.shape, whole.dtype),
        in_specs=[pl.BlockSpec(memory_space=pltpu.VMEM)] * len(pieces) + [pl.BlockSpec(memory_space=pl.ANY)],
        out_specs=pl.BlockSpec(memory_space=pl.ANY),
        scratch_shapes=[pltpu.SemaphoreType.DMA((len(hops),))],
        input_output_aliases={len(pieces): 0},
        compiler_params=pltpu.CompilerParams(vmem_limit_bytes=8 << 20),
        cost_estimate=pl.CostEstimate(flops=0, bytes_accessed=4 * sum(p.size for p in pieces), transcendentals=0),
    )(*pieces, whole)


def split_kernel(start, groups, axis, *refs):
    pieces, (out_ref, away_ref, sems) = refs[: len(CHIPS)], refs[-3:]
    me = lax.axis_index(axis) if axis else 0
    core = me % 2
    rows = out_ref.shape[0]
    stores = []
    for i, chip in enumerate(CHIPS):
        kept = pieces[i].at[pl.ds(pl.multiple_of(core * rows, rows), rows)]
        stores.append(place(me, groups, start, kept, (chip, 0), out_ref, sems.at[i]))
        stores[i].start()
    for i in range(len(CHIPS)):
        away_ref[i * rows : (i + 1) * rows] = pieces[i][pl.ds(pl.multiple_of((1 - core) * rows, rows), rows)]
    for store in stores:
        store.wait()


def split(start, span, groups, pieces, axis="el"):
    rows, width = pieces[0].shape[0] // 2, pieces[0].shape[1]
    dtype = pieces[0].dtype
    return pl.pallas_call(
        functools.partial(split_kernel, start, groups, axis),
        out_shape=[
            jax.ShapeDtypeStruct((rows, groups * span), dtype),
            jax.ShapeDtypeStruct((len(CHIPS) * rows, width), dtype),
        ],
        in_specs=[pl.BlockSpec(memory_space=pltpu.VMEM)] * len(pieces),
        out_specs=[pl.BlockSpec(memory_space=pl.ANY), pl.BlockSpec(memory_space=pltpu.VMEM)],
        scratch_shapes=[pltpu.SemaphoreType.DMA((len(CHIPS),))],
        compiler_params=pltpu.CompilerParams(vmem_limit_bytes=8 << 20),
        cost_estimate=pl.CostEstimate(flops=0, bytes_accessed=4 * sum(p.size for p in pieces), transcendentals=0),
    )(*pieces)


def send(piece, groups, hop):
    if hop == (0, 0):
        return piece
    pairs = [(i, (i // 2 + hop[0]) % (groups // 2) * 2 + (i + hop[1]) % 2) for i in range(groups)]
    return lax.ppermute(piece, "el", pairs)


def on_device(field_points, owner_map, send_counts, tile_rows, tile_cols, weights):
    elems, points, channels = field_points.shape
    devices = lax.axis_size(("el", "tg"))
    groups = lax.axis_size("el")
    packed = pack(owner_map, send_counts, field_points)
    outgoing = packed.reshape(devices, elems // devices * points, channels)
    incoming = lax.all_to_all(outgoing, ("el", "tg"), split_axis=0, concat_axis=0, tiled=True)
    ready = stage(tile_rows, weights)
    source = incoming.reshape(-1, weights.shape[-1], channels)
    targets, tile = weights.shape[1], weights.shape[-1]
    count = targets * SHARES[0] // sum(SHARES)
    *pieces, source = remap(0, count, True, tile_rows, tile_cols, weights, source, ready)
    received = [send(piece, groups, hop) for piece, hop in zip(pieces, HOPS_OF[True])]
    pieces = remap(count, targets - count, False, tile_rows, tile_cols, weights, source)
    whole, away = split(0, targets * tile, groups, received)
    away = send(away, groups, (0, 1))
    received = [send(piece, groups, hop) for piece, hop in zip(pieces, HOPS)]
    whole = join(0, tuple((chip, 1) for chip in CHIPS), groups, [away], whole)
    whole = join(count * tile, HOPS, groups, received, whole)
    return whole


def solution(mesh):
    return jax.shard_map(
        on_device,
        mesh=mesh,
        in_specs=(
            P(("el", "tg"), None, None),
            P(("el", "tg"), None),
            P(("el", "tg"), None),
            P(("el", "tg"), None),
            P(("el", "tg"), None, None),
            P(("el", "tg"), None, None, None, None),
        ),
        out_specs=P("el", "tg"),
        check_vma=False,
    )
```

profile of v0, /device:TPU:1, one launch (start us, length us, event | category | flops | bytes accessed | tf_op | source)
XLA Modules:
  0.0 115.7 jit_solution(15001780375891189661)
XLA Ops:
  0.0 5.1 %pack.1 = bf16[512,16,256]{2,1,0:T(8,128)(2,1)} custom-call(s32[1,512]{1,0:T(1,128)} %owner_ref.1, s32[1,512]{1,0:T(1,128)} %counts_ref.1, bf16[512,16,256]{2,1,0:T(8,128)(2,1)} %field_ref.1), custom_call_target="tpu_custom_call" | custom-call | tf_op jit(solution)/shard_map/pack/pallas_call | solution.py:50
  5.2 12.0 %all-to-all-start = ((bf16[128,64,256]{2,1,0:T(8,128)(2,1)}), bf16[128,64,256]{2,1,0:T(8,128)(2,1)}, u32[]{:S(2)}, u32[]{:S(2)}) async-start(bf16[128,64,256]{2,1,0:T(8,128)(2,1)} %bitcast.2), calls=%async_computation | async-start | bytes 8388608 | tf_op jit(solution)/shard_map/all_to_all | solution.py:253
  17.2 2.5 %stage.1.refs_0_ = bf16[6,16,128,128]{3,2,1,0:T(8,128)(2,1)S(1)} custom-call(s32[1,32]{1,0:T(1,128)S(1)} %copy-done, bf16[1,32,16,128,128]{4,3,2,1,0:T(8,128)(2,1)} %w_ref.5), custom_call_target="tpu_custom_call" | custom-call | bytes 6291456 | tf_op jit(solution)/shard_map/stage/pallas_call | solution.py:87
  19.7 49.4 %all-to-all-done = bf16[128,64,256]{2,1,0:T(8,128)(2,1)} async-done(((bf16[128,64,256]{2,1,0:T(8,128)(2,1)}), bf16[128,64,256]{2,1,0:T(8,128)(2,1)}, u32[]{:S(2)}, u32[]{:S(2)}) %all-to-all-start) | async-done | bytes 4194336 | tf_op jit(solution)/shard_map/all_to_all | solution.py:253
  69.1 6.6 %shard_map.64 = (bf16[64,1792]{1,0:T(8,128)(2,1)S(1)}, bf16[64,1792]{1,0:T(8,128)(2,1)S(1)}, bf16[64,1792]{1,0:T(8,128)(2,1)S(1)}, bf16[64,1792]{1,0:T(8,128)(2,1)S(1)}, bf16[64,128,256]{2,1,0:T(8,128)(2,1)S(1)}) custom-call(s32[1,32]{1,0:T(1,128)S(1)} %copy-done, s32[1,32,16]{2,1,0:T(8,128)S(1)} %copy.10.cols_ref, bf16[1,32,16,128,128]{4,3,2,1,0:T(8,128)(2,1)} %w_ref.5, ...), custom_call_target="tpu_custom_call" | custom-call | flops 1879048192 | bytes 11534336 | tf_op jit(solution)/shard_map/pallas_call | solution.py:153
  75.7 3.0 %collective-permute-start.7 = (bf16[64,1792]{1,0:T(8,128)(2,1)S(1)}, bf16[64,1792]{1,0:T(8,128)(2,1)S(1)}, u32[]{:S(2)}, u32[]{:S(2)}) collective-permute-start(bf16[64,1792]{1,0:T(8,128)(2,1)S(1)} %get-tuple-element.29), channel_id=1, source_target_pairs={{0,64},{16,80},{32,96},{48,112},{64,0},{80,16},{96,32},{112,48},{1... | collective-permute-start | bytes 688136 | tf_op jit(solution)/shard_map/ppermute | solution.py:244
  79.0 2.3 %collective-permute-start.9 = (bf16[64,1792]{1,0:T(8,128)(2,1)S(1)}, bf16[64,1792]{1,0:T(8,128)(2,1)S(1)}, u32[]{:S(2)}, u32[]{:S(2)}) collective-permute-start(bf16[64,1792]{1,0:T(8,128)(2,1)S(1)} %get-tuple-element.31), channel_id=1, source_target_pairs={{0,96},{16,112},{32,0},{48,16},{64,32},{80,48},{96,64},{112,80},{1... | collective-permute-start | bytes 688136 | tf_op jit(solution)/shard_map/ppermute | solution.py:244
  81.3 1.6 %collective-permute-done.7.refs_0_ = bf16[64,1792]{1,0:T(8,128)(2,1)S(1)} collective-permute-done((bf16[64,1792]{1,0:T(8,128)(2,1)S(1)}, bf16[64,1792]{1,0:T(8,128)(2,1)S(1)}, u32[]{:S(2)}, u32[]{:S(2)}) %collective-permute-start.7) | collective-permute-done | bytes 229408 | tf_op jit(solution)/shard_map/ppermute | solution.py:244
  83.0 6.2 %collective-permute-done.8.refs_1_ = bf16[64,1792]{1,0:T(8,128)(2,1)S(1)} collective-permute-done((bf16[64,1792]{1,0:T(8,128)(2,1)S(1)}, bf16[64,1792]{1,0:T(8,128)(2,1)S(1)}, u32[]{:S(2)}, u32[]{:S(2)}) %collective-permute-start.8) | collective-permute-done | bytes 229408 | tf_op jit(solution)/shard_map/ppermute | solution.py:244
  89.2 0.8 shard_map.66
  90.0 1.4 %collective-permute-start.10 = (bf16[128,1792]{1,0:T(8,128)(2,1)S(1)}, bf16[128,1792]{1,0:T(8,128)(2,1)S(1)}, u32[]{:S(2)}, u32[]{:S(2)}) collective-permute-start(bf16[128,1792]{1,0:T(8,128)(2,1)S(1)} %get-tuple-element.33), channel_id=1, source_target_pairs={{0,16},{16,0},{32,48},{48,32},{64,80},{80,64},{96,112},{112,96},{1... | collective-permute-start | bytes 1376264 | tf_op jit(solution)/shard_map/ppermute | solution.py:244
  91.4 6.4 %shard_map.65 = (bf16[32,2304]{1,0:T(8,128)(2,1)S(1)}, bf16[32,2304]{1,0:T(8,128)(2,1)S(1)}, bf16[32,2304]{1,0:T(8,128)(2,1)S(1)}, bf16[32,2304]{1,0:T(8,128)(2,...) custom-call(s32[1,32]{1,0:T(1,128)S(1)} %copy-done, ...), custom_call_target="tpu_custom_call" | custom-call | flops 2415919104 | bytes 13631488 | tf_op jit(solution)/shard_map/pallas_call | solution.py:153
  97.8 1.9 %collective-permute-start = (bf16[32,2304]{1,0:T(8,128)(2,1)S(1)}, bf16[32,2304]{1,0:T(8,128)(2,1)S(1)}, u32[]{:S(2)}, u32[]{:S(2)}) collective-permute-start(bf16[32,2304]{1,0:T(8,128)(2,1)S(1)} %get-tuple-element.21), channel_id=1, source_target_pairs={{0,64},{16,80},{32,96},{48,112},{64,0},{80,16},{96,32},{112,48},{1... | collective-permute-start | bytes 442376 | tf_op jit(solution)/shard_map/ppermute | solution.py:244
  99.6 1.4 %collective-permute-start.1 = (bf16[32,2304]{1,0:T(8,128)(2,1)S(1)}, bf16[32,2304]{1,0:T(8,128)(2,1)S(1)}, u32[]{:S(2)}, u32[]{:S(2)}) collective-permute-start(bf16[32,2304]{1,0:T(8,128)(2,1)S(1)} %get-tuple-element.22), channel_id=1, source_target_pairs={{0,80},{16,64},{32,112},{48,96},{64,16},{80,0},{96,48},{112,32},{1... | collective-permute-start | bytes 442376 | tf_op jit(solution)/shard_map/ppermute | solution.py:244
  101.0 1.2 %collective-permute-start.2 = (bf16[32,2304]{1,0:T(8,128)(2,1)S(1)}, bf16[32,2304]{1,0:T(8,128)(2,1)S(1)}, u32[]{:S(2)}, u32[]{:S(2)}) collective-permute-start(bf16[32,2304]{1,0:T(8,128)(2,1)S(1)} %get-tuple-element.23), channel_id=1, source_target_pairs={{0,32},{16,48},{32,64},{48,80},{64,96},{80,112},{96,0},{112,16},{1... | collective-permute-start | bytes 442376 | tf_op jit(solution)/shard_map/ppermute | solution.py:244
  102.2 1.5 %collective-permute-start.3 = (bf16[32,2304]{1,0:T(8,128)(2,1)S(1)}, bf16[32,2304]{1,0:T(8,128)(2,1)S(1)}, u32[]{:S(2)}, u32[]{:S(2)}) collective-permute-start(bf16[32,2304]{1,0:T(8,128)(2,1)S(1)} %get-tuple-element.24), channel_id=1, source_target_pairs={{0,96},{16,112},{32,0},{48,16},{64,32},{80,48},{96,64},{112,80},{1... | collective-permute-start | bytes 442376 | tf_op jit(solution)/shard_map/ppermute | solution.py:244
  103.7 1.1 collective-permute-done.refs_0_
  104.7 2.5 %collective-permute-start.4 = (bf16[32,2304]{1,0:T(8,128)(2,1)S(1)}, bf16[32,2304]{1,0:T(8,128)(2,1)S(1)}, u32[]{:S(2)}, u32[]{:S(2)}) collective-permute-start(bf16[32,2304]{1,0:T(8,128)(2,1)S(1)} %get-tuple-element.25), channel_id=1, source_target_pairs={{0,48},{16,32},{32,80},{48,64},{64,112},{80,96},{96,16},{112,0},{1... | collective-permute-start | bytes 442376 | tf_op jit(solution)/shard_map/ppermute | solution.py:244
  107.2 1.4 %collective-permute-done.1.refs_1_ = bf16[32,2304]{1,0:T(8,128)(2,1)S(1)} collective-permute-done((bf16[32,2304]{1,0:T(8,128)(2,1)S(1)}, bf16[32,2304]{1,0:T(8,128)(2,1)S(1)}, u32[]{:S(2)}, u32[]{:S(2)}) %collective-permute-start.1) | collective-permute-done | bytes 147488 | tf_op jit(solution)/shard_map/ppermute | solution.py:244
  108.6 2.1 %collective-permute-start.5 = (bf16[32,2304]{1,0:T(8,128)(2,1)S(1)}, bf16[32,2304]{1,0:T(8,128)(2,1)S(1)}, u32[]{:S(2)}, u32[]{:S(2)}) collective-permute-start(bf16[32,2304]{1,0:T(8,128)(2,1)S(1)} %get-tuple-element.26), channel_id=1, source_target_pairs={{0,112},{16,96},{32,16},{48,0},{64,48},{80,32},{96,80},{112,64},{1... | collective-permute-start | bytes 442376 | tf_op jit(solution)/shard_map/ppermute | solution.py:244
  110.7 0.7 collective-permute-start.6
  111.4 0.8 shard_map.67.refs_8_
  112.2 2.4 %collective-permute-done.4.refs_4_ = bf16[32,2304]{1,0:T(8,128)(2,1)S(1)} collective-permute-done((bf16[32,2304]{1,0:T(8,128)(2,1)S(1)}, bf16[32,2304]{1,0:T(8,128)(2,1)S(1)}, u32[]{:S(2)}, u32[]{:S(2)}) %collective-permute-start.4) | collective-permute-done | bytes 147488 | tf_op jit(solution)/shard_map/ppermute | solution.py:244
  114.6 1.1 shard_map.68
  (12 shorter events, 0.5 us)
Async XLA Ops:
  5.2 12.0 %copy-start.1 = (s32[1,32,16]{1,2,0:T(8,128)S(1)}, s32[1,32,16]{1,2,0:T(8,128)}, u32[]{:S(2)}) copy-start(s32[1,32,16]{1,2,0:T(8,128)} %param.10) | copy-start | bytes 6148
  5.2 12.1 %copy-start = (s32[1,32]{1,0:T(1,128)S(1)}, s32[1,32]{1,0:T(1,128)}, u32[]{:S(2)}) copy-start(s32[1,32]{1,0:T(1,128)} %rows_ref.5) | copy-start | bytes 388
  5.2 63.9 %all-to-all-start = ((bf16[128,64,256]{2,1,0:T(8,128)(2,1)}), bf16[128,64,256]{2,1,0:T(8,128)(2,1)}, u32[]{:S(2)}, u32[]{:S(2)}) async-start(bf16[128,64,256]{2,1,0:T(8,128)(2,1)} %bitcast.2), calls=%async_computation | async-start | bytes 8388608 | tf_op jit(solution)/shard_map/all_to_all | solution.py:253
  75.7 7.3 %collective-permute-start.7 = (bf16[64,1792]{1,0:T(8,128)(2,1)S(1)}, bf16[64,1792]{1,0:T(8,128)(2,1)S(1)}, u32[]{:S(2)}, u32[]{:S(2)}) collective-permute-start(bf16[64,1792]{1,0:T(8,128)(2,1)S(1)} %get-tuple-element.29), channel_id=1, source_target_pairs={{0,64},{16,80},{32,96},{48,112},{64,0},{80,16},{96,32},{112,48},{1... | collective-permute-start | bytes 688136 | tf_op jit(solution)/shard_map/ppermute | solution.py:244
  78.7 10.5 %collective-permute-start.8 = (bf16[64,1792]{1,0:T(8,128)(2,1)S(1)}, bf16[64,1792]{1,0:T(8,128)(2,1)S(1)}, u32[]{:S(2)}, u32[]{:S(2)}) collective-permute-start(bf16[64,1792]{1,0:T(8,128)(2,1)S(1)} %get-tuple-element.30), channel_id=1, source_target_pairs={{0,32},{16,48},{32,64},{48,80},{64,96},{80,112},{96,0},{112,16},{1... | collective-permute-start | bytes 688136 | tf_op jit(solution)/shard_map/ppermute | solution.py:244
  79.0 10.2 %collective-permute-start.9 = (bf16[64,1792]{1,0:T(8,128)(2,1)S(1)}, bf16[64,1792]{1,0:T(8,128)(2,1)S(1)}, u32[]{:S(2)}, u32[]{:S(2)}) collective-permute-start(bf16[64,1792]{1,0:T(8,128)(2,1)S(1)} %get-tuple-element.31), channel_id=1, source_target_pairs={{0,96},{16,112},{32,0},{48,16},{64,32},{80,48},{96,64},{112,80},{1... | collective-permute-start | bytes 688136 | tf_op jit(solution)/shard_map/ppermute | solution.py:244
  90.0 20.7 %collective-permute-start.10 = (bf16[128,1792]{1,0:T(8,128)(2,1)S(1)}, bf16[128,1792]{1,0:T(8,128)(2,1)S(1)}, u32[]{:S(2)}, u32[]{:S(2)}) collective-permute-start(bf16[128,1792]{1,0:T(8,128)(2,1)S(1)} %get-tuple-element.33), channel_id=1, source_target_pairs={{0,16},{16,0},{32,48},{48,32},{64,80},{80,64},{96,112},{112,96},{1... | collective-permute-start | bytes 1376264 | tf_op jit(solution)/shard_map/ppermute | solution.py:244
  97.8 7.0 %collective-permute-start = (bf16[32,2304]{1,0:T(8,128)(2,1)S(1)}, bf16[32,2304]{1,0:T(8,128)(2,1)S(1)}, u32[]{:S(2)}, u32[]{:S(2)}) collective-permute-start(bf16[32,2304]{1,0:T(8,128)(2,1)S(1)} %get-tuple-element.21), channel_id=1, source_target_pairs={{0,64},{16,80},{32,96},{48,112},{64,0},{80,16},{96,32},{112,48},{1... | collective-permute-start | bytes 442376 | tf_op jit(solution)/shard_map/ppermute | solution.py:244
  99.6 9.0 %collective-permute-start.1 = (bf16[32,2304]{1,0:T(8,128)(2,1)S(1)}, bf16[32,2304]{1,0:T(8,128)(2,1)S(1)}, u32[]{:S(2)}, u32[]{:S(2)}) collective-permute-start(bf16[32,2304]{1,0:T(8,128)(2,1)S(1)} %get-tuple-element.22), channel_id=1, source_target_pairs={{0,80},{16,64},{32,112},{48,96},{64,16},{80,0},{96,48},{112,32},{1... | collective-permute-start | bytes 442376 | tf_op jit(solution)/shard_map/ppermute | solution.py:244
  101.0 11.2 %collective-permute-start.2 = (bf16[32,2304]{1,0:T(8,128)(2,1)S(1)}, bf16[32,2304]{1,0:T(8,128)(2,1)S(1)}, u32[]{:S(2)}, u32[]{:S(2)}) collective-permute-start(bf16[32,2304]{1,0:T(8,128)(2,1)S(1)} %get-tuple-element.23), channel_id=1, source_target_pairs={{0,32},{16,48},{32,64},{48,80},{64,96},{80,112},{96,0},{112,16},{1... | collective-permute-start | bytes 442376 | tf_op jit(solution)/shard_map/ppermute | solution.py:244
  102.2 10.0 %collective-permute-start.3 = (bf16[32,2304]{1,0:T(8,128)(2,1)S(1)}, bf16[32,2304]{1,0:T(8,128)(2,1)S(1)}, u32[]{:S(2)}, u32[]{:S(2)}) collective-permute-start(bf16[32,2304]{1,0:T(8,128)(2,1)S(1)} %get-tuple-element.24), channel_id=1, source_target_pairs={{0,96},{16,112},{32,0},{48,16},{64,32},{80,48},{96,64},{112,80},{1... | collective-permute-start | bytes 442376 | tf_op jit(solution)/shard_map/ppermute | solution.py:244
  104.7 9.9 %collective-permute-start.4 = (bf16[32,2304]{1,0:T(8,128)(2,1)S(1)}, bf16[32,2304]{1,0:T(8,128)(2,1)S(1)}, u32[]{:S(2)}, u32[]{:S(2)}) collective-permute-start(bf16[32,2304]{1,0:T(8,128)(2,1)S(1)} %get-tuple-element.25), channel_id=1, source_target_pairs={{0,48},{16,32},{32,80},{48,64},{64,112},{80,96},{96,16},{112,0},{1... | collective-permute-start | bytes 442376 | tf_op jit(solution)/shard_map/ppermute | solution.py:244
  108.6 6.0 %collective-permute-start.5 = (bf16[32,2304]{1,0:T(8,128)(2,1)S(1)}, bf16[32,2304]{1,0:T(8,128)(2,1)S(1)}, u32[]{:S(2)}, u32[]{:S(2)}) collective-permute-start(bf16[32,2304]{1,0:T(8,128)(2,1)S(1)} %get-tuple-element.26), channel_id=1, source_target_pairs={{0,112},{16,96},{32,16},{48,0},{64,48},{80,32},{96,80},{112,64},{1... | collective-permute-start | bytes 442376 | tf_op jit(solution)/shard_map/ppermute | solution.py:244
  110.7 4.0 %collective-permute-start.6 = (bf16[32,2304]{1,0:T(8,128)(2,1)S(1)}, bf16[32,2304]{1,0:T(8,128)(2,1)S(1)}, u32[]{:S(2)}, u32[]{:S(2)}) collective-permute-start(bf16[32,2304]{1,0:T(8,128)(2,1)S(1)} %get-tuple-element.27), channel_id=1, source_target_pairs={{0,16},{16,0},{32,48},{48,32},{64,80},{80,64},{96,112},{112,96},{1... | collective-permute-start | bytes 442376 | tf_op jit(solution)/shard_map/ppermute | solution.py:244
where the time goes:
time: 116 us
  waiting for transfers between devices  62.1 us (54%)
  starting transfers between devices  30.2 us (26%)
  Pallas kernels  23.3 us (20%)
    all_to_all x1, waiting for transfers between devices, on_device(): lax.all_to_all(outgoing, ('el', 'tg'), split_axis=0, concat_axis=0, tiled...  49.4 us
    ppermute x11, starting transfers between devices, send(): return lax.ppermute(piece, 'el', pairs)  18.2 us
    pallas_call x2, Pallas kernels, remap(): pl.pallas_call(functools.partial(remap_kernel, first, staged, paired, axi...  13 us
    ppermute x11, waiting for transfers between devices, send(): return lax.ppermute(piece, 'el', pairs)  12.7 us
    all_to_all x1, starting transfers between devices, on_device(): lax.all_to_all(outgoing, ('el', 'tg'), split_axis=0, concat_axis=0, tiled...  12 us
    pallas_call x1, Pallas kernels, pack(): pl.pallas_call(functools.partial(pack_kernel, chunks), out_shape=jax.Shap...  5.15 us
    pallas_call x1, Pallas kernels, stage(): pl.pallas_call(stage_kernel, out_shape=jax.ShapeDtypeStruct((STAGED, *wei...  2.46 us
  transfers between devices with their start and end apart: 12, of which 6 were waited for; matrix products, arithmetic and copies ran while one was open for 0% of the time, Pallas kernels for 8%

commit v1 on v0

--- a/solution.py
+++ b/solution.py
@@ -9,7 +9,9 @@
 
 SHARES = (7, 9)
 STAGED = 6
-CHIPS = (2, 1, 3, 0)
+CHIPS = (1, 3, 2, 0)
+EARLY = (0, 1, 2, 3, 6, 7)
+LATE = (4, 5)
 GROUP = 4
 AHEAD = 2
 HOPS = ((2, 0), (2, 1), (1, 0), (3, 0), (1, 1), (3, 1), (0, 1), (0, 0))
@@ -19,8 +21,10 @@
     elems, points, channels = dst.shape
     step = elems // chunks
     owners = elems // 4
+
     def fetch(c):
         return pltpu.make_async_copy(field_ref.at[pl.ds(c * step, step)], buf.at[pl.ds(c * step, step)], sem_in.at[c])
+
     for c in range(chunks):
         fetch(c).start()
     owner = owner_ref[...]
@@ -36,10 +40,12 @@
     point = lax.broadcasted_iota(jnp.int32, (points, channels), 0)
     for c in range(chunks):
         fetch(c).wait()
+
         def body(e, carry):
             live = point < counts_ref[0, e]
             dst[pos_s[0, e]] = jnp.where(live, buf[e], jnp.zeros((), buf.dtype))
             return carry
+
         lax.fori_loop(c * step, (c + 1) * step, body, 0, unroll=8)
     out = pltpu.make_async_copy(dst, out_ref, sem_out)
     out.start()
@@ -118,13 +124,27 @@
 
     for q in range(staged, GROUP * AHEAD):
         fetch(q).start()
+    me = lax.axis_index(axis) if axis else 0
+    places = [peer(me, groups, hop) // 2 * 2 if paired else peer(me, groups, hop) for hop in HOPS_OF[paired]]
+
+    def hand_out(g):
+        lanes = slice(g * tile, min(count, g + GROUP) * tile)
+        for piece, row in zip(outs, places):
+            piece[:, lanes] = out[pl.ds(pl.multiple_of(row * rows, rows), piece.shape[0]), lanes]
+
+    ahead = GROUP * AHEAD
     if staged:
         load.wait()
+        for q in range(ahead, ahead + GROUP):
+            fetch(q).start()
+        ahead += GROUP
     for g in range(0, count, GROUP):
         for q in range(max(g, staged), min(count, g + GROUP)):
             fetch(q).wait()
-        for q in range(g + GROUP * AHEAD, min(count, g + GROUP * AHEAD + GROUP)):
+        for q in range(g + ahead, min(count, g + ahead + GROUP)):
             fetch(q).start()
+        if g:
+            hand_out(g - GROUP)
         for q in range(g, min(count, g + GROUP)):
             t = order[first + q]
             total = None
@@ -134,10 +154,7 @@
                 r = jnp.dot(w, x, preferred_element_type=jnp.float32)
                 total = r if total is None else total + r
             out[:, q * tile : (q + 1) * tile] = total.T.astype(out.dtype)
-    me = lax.axis_index(axis) if axis else 0
-    for piece, hop in zip(outs, HOPS_OF[paired]):
-        row = peer(me, groups, hop) // 2 * 2 if paired else peer(me, groups, hop)
-        piece[...] = out[pl.ds(pl.multiple_of(row * rows, rows), piece.shape[0])]
+    hand_out(count - 1 - (count - 1) % GROUP)
 
 
 def remap(first, count, paired, tile_rows, tile_cols, weights, source, ready=None, axis="el"):
@@ -184,7 +201,7 @@
     rows = out_ref.shape[0]
     stores = []
     for i, hop in enumerate(hops):
-        piece = refs[i] if len(hops) == groups else refs[0].at[pl.ds(i * rows, rows)]
+        piece = refs[i] if len(refs) > 4 else refs[0].at[pl.ds(i * rows, rows)]
         stores.append(place(me, groups, start, piece, hop, out_ref, sems.at[i]))
         stores[i].start()
     for store in stores:
@@ -262,7 +279,8 @@
     away = send(away, groups, (0, 1))
     received = [send(piece, groups, hop) for piece, hop in zip(pieces, HOPS)]
     whole = join(0, tuple((chip, 1) for chip in CHIPS), groups, [away], whole)
-    whole = join(count * tile, HOPS, groups, received, whole)
+    whole = join(count * tile, tuple(HOPS[n] for n in EARLY), groups, [received[n] for n in EARLY], whole)
+    whole = join(count * tile, tuple(HOPS[n] for n in LATE), groups, [received[n] for n in LATE], whole)
     return whole
 
 

time: 116 us -> 117 us (level)
  waiting for transfers between devices: 62.1 us -> 63.5 us
    ppermute x11, waiting for transfers between devices: 12.7 us -> 14.2 us  [send(): return lax.ppermute(piece, 'el', pairs)]
    pallas_call x2 -> x3, Pallas kernels: 1.86 us -> 2.5 us  [join(): pl.pallas_call(functools.partial(join_kernel, start, groups, hops, axis),...]
  transfers between devices with their start and end apart: 12 -> 12, of which waited for: 6 -> 8; matrix products, arithmetic and copies ran while one was open for 0% -> 0% of each run, Pallas kernels for 8% -> 9%
where the time goes in v1:
time: 117 us
  waiting for transfers between devices  63.5 us (54%)
  starting transfers between devices  29.2 us (25%)
  Pallas kernels  24 us (21%)
    all_to_all x1, waiting for transfers between devices, on_device(): lax.all_to_all(outgoing, ('el', 'tg'), split_axis=0, concat_axis=0, tiled...  49.4 us
    ppermute x11, starting transfers between devices, send(): return lax.ppermute(piece, 'el', pairs)  17.2 us
    ppermute x11, waiting for transfers between devices, send(): return lax.ppermute(piece, 'el', pairs)  14.2 us
    pallas_call x2, Pallas kernels, remap(): pl.pallas_call(functools.partial(remap_kernel, first, staged, paired, axi...  13.1 us
    all_to_all x1, starting transfers between devices, on_device(): lax.all_to_all(outgoing, ('el', 'tg'), split_axis=0, concat_axis=0, tiled...  12 us
    pallas_call x1, Pallas kernels, pack(): pl.pallas_call(functools.partial(pack_kernel, chunks), out_shape=jax.Shap...  5.15 us
    pallas_call x3, Pallas kernels, join(): pl.pallas_call(functools.partial(join_kernel, start, groups, hops, axis),...  2.5 us
    pallas_call x1, Pallas kernels, stage(): pl.pallas_call(stage_kernel, out_shape=jax.ShapeDtypeStruct((STAGED, *wei...  2.46 us
  transfers between devices with their start and end apart: 12, of which 8 were waited for; matrix products, arithmetic and copies ran while one was open for 0% of the time, Pallas kernels for 9%

profile of v1, /device:TPU:1, one launch (start us, length us, event | category | flops | bytes accessed | tf_op | source)
XLA Modules:
  0.0 117.0 jit_solution(8837125959524188713)
XLA Ops:
  0.0 5.1 %pack.1 = bf16[512,16,256]{2,1,0:T(8,128)(2,1)} custom-call(s32[1,512]{1,0:T(1,128)} %owner_ref.1, s32[1,512]{1,0:T(1,128)} %counts_ref.1, bf16[512,16,256]{2,1,0:T(8,128)(2,1)} %field_ref.1), custom_call_target="tpu_custom_call" | custom-call | tf_op jit(solution)/shard_map/pack/pallas_call | solution.py:56
  5.2 12.0 %all-to-all-start = ((bf16[128,64,256]{2,1,0:T(8,128)(2,1)}), bf16[128,64,256]{2,1,0:T(8,128)(2,1)}, u32[]{:S(2)}, u32[]{:S(2)}) async-start(bf16[128,64,256]{2,1,0:T(8,128)(2,1)} %bitcast.2), calls=%async_computation | async-start | bytes 8388608 | tf_op jit(solution)/shard_map/all_to_all | solution.py:270
  17.2 2.5 %stage.1.refs_0_ = bf16[6,16,128,128]{3,2,1,0:T(8,128)(2,1)S(1)} custom-call(s32[1,32]{1,0:T(1,128)S(1)} %copy-done, bf16[1,32,16,128,128]{4,3,2,1,0:T(8,128)(2,1)} %w_ref.5), custom_call_target="tpu_custom_call" | custom-call | bytes 6291456 | tf_op jit(solution)/shard_map/stage/pallas_call | solution.py:93
  19.7 49.4 %all-to-all-done = bf16[128,64,256]{2,1,0:T(8,128)(2,1)} async-done(((bf16[128,64,256]{2,1,0:T(8,128)(2,1)}), bf16[128,64,256]{2,1,0:T(8,128)(2,1)}, u32[]{:S(2)}, u32[]{:S(2)}) %all-to-all-start) | async-done | bytes 4194336 | tf_op jit(solution)/shard_map/all_to_all | solution.py:270
  69.1 6.6 %shard_map.64 = (bf16[64,1792]{1,0:T(8,128)(2,1)S(1)}, bf16[64,1792]{1,0:T(8,128)(2,1)S(1)}, bf16[64,1792]{1,0:T(8,128)(2,1)S(1)}, bf16[64,1792]{1,0:T(8,128)(2,1)S(1)}, bf16[64,128,256]{2,1,0:T(8,128)(2,1)S(1)}) custom-call(s32[1,32]{1,0:T(1,128)S(1)} %copy-done, s32[1,32,16]{2,1,0:T(8,128)S(1)} %copy.11.cols_ref, bf16[1,32,16,128,128]{4,3,2,1,0:T(8,128)(2,1)} %w_ref.5, ...), custom_call_target="tpu_custom_call" | custom-call | flops 1879048192 | bytes 11534336 | tf_op jit(solution)/shard_map/pallas_call | solution.py:170
  75.8 2.7 %collective-permute-start.8 = (bf16[64,1792]{1,0:T(8,128)(2,1)S(1)}, bf16[64,1792]{1,0:T(8,128)(2,1)S(1)}, u32[]{:S(2)}, u32[]{:S(2)}) collective-permute-start(bf16[64,1792]{1,0:T(8,128)(2,1)S(1)} %get-tuple-element.30), channel_id=1, source_target_pairs={{0,96},{16,112},{32,0},{48,16},{64,32},{80,48},{96,64},{112,80},{1... | collective-permute-start | bytes 688136 | tf_op jit(solution)/shard_map/ppermute | solution.py:261
  78.5 1.6 %collective-permute-start.9 = (bf16[64,1792]{1,0:T(8,128)(2,1)S(1)}, bf16[64,1792]{1,0:T(8,128)(2,1)S(1)}, u32[]{:S(2)}, u32[]{:S(2)}) collective-permute-start(bf16[64,1792]{1,0:T(8,128)(2,1)S(1)} %get-tuple-element.31), channel_id=1, source_target_pairs={{0,64},{16,80},{32,96},{48,112},{64,0},{80,16},{96,32},{112,48},{1... | collective-permute-start | bytes 688136 | tf_op jit(solution)/shard_map/ppermute | solution.py:261
  80.1 2.6 %collective-permute-done.7.refs_0_ = bf16[64,1792]{1,0:T(8,128)(2,1)S(1)} collective-permute-done((bf16[64,1792]{1,0:T(8,128)(2,1)S(1)}, bf16[64,1792]{1,0:T(8,128)(2,1)S(1)}, u32[]{:S(2)}, u32[]{:S(2)}) %collective-permute-start.7) | collective-permute-done | bytes 229408 | tf_op jit(solution)/shard_map/ppermute | solution.py:261
  83.2 5.5 %collective-permute-done.9.refs_2_ = bf16[64,1792]{1,0:T(8,128)(2,1)S(1)} collective-permute-done((bf16[64,1792]{1,0:T(8,128)(2,1)S(1)}, bf16[64,1792]{1,0:T(8,128)(2,1)S(1)}, u32[]{:S(2)}, u32[]{:S(2)}) %collective-permute-start.9) | collective-permute-done | bytes 229408 | tf_op jit(solution)/shard_map/ppermute | solution.py:261
  88.7 0.8 shard_map.66
  89.5 2.5 %collective-permute-start.10 = (bf16[128,1792]{1,0:T(8,128)(2,1)S(1)}, bf16[128,1792]{1,0:T(8,128)(2,1)S(1)}, u32[]{:S(2)}, u32[]{:S(2)}) collective-permute-start(bf16[128,1792]{1,0:T(8,128)(2,1)S(1)} %get-tuple-element.33), channel_id=1, source_target_pairs={{0,16},{16,0},{32,48},{48,32},{64,80},{80,64},{96,112},{112,96},{1... | collective-permute-start | bytes 1376264 | tf_op jit(solution)/shard_map/ppermute | solution.py:261
  92.0 6.5 %shard_map.65 = (bf16[32,2304]{1,0:T(8,128)(2,1)S(1)}, bf16[32,2304]{1,0:T(8,128)(2,1)S(1)}, bf16[32,2304]{1,0:T(8,128)(2,1)S(1)}, bf16[32,2304]{1,0:T(8,128)(2,...) custom-call(s32[1,32]{1,0:T(1,128)S(1)} %copy-done, ...), custom_call_target="tpu_custom_call" | custom-call | flops 2415919104 | bytes 13631488 | tf_op jit(solution)/shard_map/pallas_call | solution.py:170
  98.5 0.6 collective-permute-start.2
  99.1 2.6 %collective-permute-start.3 = (bf16[32,2304]{1,0:T(8,128)(2,1)S(1)}, bf16[32,2304]{1,0:T(8,128)(2,1)S(1)}, u32[]{:S(2)}, u32[]{:S(2)}) collective-permute-start(bf16[32,2304]{1,0:T(8,128)(2,1)S(1)} %get-tuple-element.24), channel_id=1, source_target_pairs={{0,80},{16,64},{32,112},{48,96},{64,16},{80,0},{96,48},{112,32},{1... | collective-permute-start | bytes 442376 | tf_op jit(solution)/shard_map/ppermute | solution.py:261
  101.7 0.9 collective-permute-start.4
  102.6 1.8 %collective-permute-start.5 = (bf16[32,2304]{1,0:T(8,128)(2,1)S(1)}, bf16[32,2304]{1,0:T(8,128)(2,1)S(1)}, u32[]{:S(2)}, u32[]{:S(2)}) collective-permute-start(bf16[32,2304]{1,0:T(8,128)(2,1)S(1)} %get-tuple-element.26), channel_id=1, source_target_pairs={{0,96},{16,112},{32,0},{48,16},{64,32},{80,48},{96,64},{112,80},{1... | collective-permute-start | bytes 442376 | tf_op jit(solution)/shard_map/ppermute | solution.py:261
  104.4 1.1 collective-permute-done.2.refs_0_
  105.5 1.4 %collective-permute-start.6 = (bf16[32,2304]{1,0:T(8,128)(2,1)S(1)}, bf16[32,2304]{1,0:T(8,128)(2,1)S(1)}, u32[]{:S(2)}, u32[]{:S(2)}) collective-permute-start(bf16[32,2304]{1,0:T(8,128)(2,1)S(1)} %get-tuple-element.27), channel_id=1, source_target_pairs={{0,16},{16,0},{32,48},{48,32},{64,80},{80,64},{96,112},{112,96},{1... | collective-permute-start | bytes 442376 | tf_op jit(solution)/shard_map/ppermute | solution.py:261
  106.9 2.4 %collective-permute-done.3.refs_1_ = bf16[32,2304]{1,0:T(8,128)(2,1)S(1)} collective-permute-done((bf16[32,2304]{1,0:T(8,128)(2,1)S(1)}, bf16[32,2304]{1,0:T(8,128)(2,1)S(1)}, u32[]{:S(2)}, u32[]{:S(2)}) %collective-permute-start.3) | collective-permute-done | bytes 147488 | tf_op jit(solution)/shard_map/ppermute | solution.py:261
  109.9 2.4 %collective-permute-start.1 = (bf16[32,2304]{1,0:T(8,128)(2,1)S(1)}, bf16[32,2304]{1,0:T(8,128)(2,1)S(1)}, u32[]{:S(2)}, u32[]{:S(2)}) collective-permute-start(bf16[32,2304]{1,0:T(8,128)(2,1)S(1)} %get-tuple-element.22), channel_id=1, source_target_pairs={{0,112},{16,96},{32,16},{48,0},{64,48},{80,32},{96,80},{112,64},{1... | collective-permute-start | bytes 442376 | tf_op jit(solution)/shard_map/ppermute | solution.py:261
  112.3 0.8 shard_map.67.refs_6_
  113.1 1.0 shard_map.68.refs_2_
  114.1 1.7 %collective-permute-done.refs_0_ = bf16[32,2304]{1,0:T(8,128)(2,1)S(1)} collective-permute-done((bf16[32,2304]{1,0:T(8,128)(2,1)S(1)}, bf16[32,2304]{1,0:T(8,128)(2,1)S(1)}, u32[]{:S(2)}, u32[]{:S(2)}) %collective-permute-start) | collective-permute-done | bytes 147488 | tf_op jit(solution)/shard_map/ppermute | solution.py:261
  116.3 0.7 shard_map.69
  (13 shorter events, 1.7 us)
Async XLA Ops:
  5.2 12.0 %copy-start.1 = (s32[1,32,16]{1,2,0:T(8,128)S(1)}, s32[1,32,16]{1,2,0:T(8,128)}, u32[]{:S(2)}) copy-start(s32[1,32,16]{1,2,0:T(8,128)} %param.10) | copy-start | bytes 6148
  5.2 12.1 %copy-start = (s32[1,32]{1,0:T(1,128)S(1)}, s32[1,32]{1,0:T(1,128)}, u32[]{:S(2)}) copy-start(s32[1,32]{1,0:T(1,128)} %rows_ref.5) | copy-start | bytes 388
  5.2 63.9 %all-to-all-start = ((bf16[128,64,256]{2,1,0:T(8,128)(2,1)}), bf16[128,64,256]{2,1,0:T(8,128)(2,1)}, u32[]{:S(2)}, u32[]{:S(2)}) async-start(bf16[128,64,256]{2,1,0:T(8,128)(2,1)} %bitcast.2), calls=%async_computation | async-start | bytes 8388608 | tf_op jit(solution)/shard_map/all_to_all | solution.py:270
  75.7 7.0 %collective-permute-start.7 = (bf16[64,1792]{1,0:T(8,128)(2,1)S(1)}, bf16[64,1792]{1,0:T(8,128)(2,1)S(1)}, u32[]{:S(2)}, u32[]{:S(2)}) collective-permute-start(bf16[64,1792]{1,0:T(8,128)(2,1)S(1)} %get-tuple-element.29), channel_id=1, source_target_pairs={{0,32},{16,48},{32,64},{48,80},{64,96},{80,112},{96,0},{112,16},{1... | collective-permute-start | bytes 688136 | tf_op jit(solution)/shard_map/ppermute | solution.py:261
  75.8 7.4 %collective-permute-start.8 = (bf16[64,1792]{1,0:T(8,128)(2,1)S(1)}, bf16[64,1792]{1,0:T(8,128)(2,1)S(1)}, u32[]{:S(2)}, u32[]{:S(2)}) collective-permute-start(bf16[64,1792]{1,0:T(8,128)(2,1)S(1)} %get-tuple-element.30), channel_id=1, source_target_pairs={{0,96},{16,112},{32,0},{48,16},{64,32},{80,48},{96,64},{112,80},{1... | collective-permute-start | bytes 688136 | tf_op jit(solution)/shard_map/ppermute | solution.py:261
  78.5 10.1 %collective-permute-start.9 = (bf16[64,1792]{1,0:T(8,128)(2,1)S(1)}, bf16[64,1792]{1,0:T(8,128)(2,1)S(1)}, u32[]{:S(2)}, u32[]{:S(2)}) collective-permute-start(bf16[64,1792]{1,0:T(8,128)(2,1)S(1)} %get-tuple-element.31), channel_id=1, source_target_pairs={{0,64},{16,80},{32,96},{48,112},{64,0},{80,16},{96,32},{112,48},{1... | collective-permute-start | bytes 688136 | tf_op jit(solution)/shard_map/ppermute | solution.py:261
  89.5 20.4 %collective-permute-start.10 = (bf16[128,1792]{1,0:T(8,128)(2,1)S(1)}, bf16[128,1792]{1,0:T(8,128)(2,1)S(1)}, u32[]{:S(2)}, u32[]{:S(2)}) collective-permute-start(bf16[128,1792]{1,0:T(8,128)(2,1)S(1)} %get-tuple-element.33), channel_id=1, source_target_pairs={{0,16},{16,0},{32,48},{48,32},{64,80},{80,64},{96,112},{112,96},{1... | collective-permute-start | bytes 1376264 | tf_op jit(solution)/shard_map/ppermute | solution.py:261
  98.5 7.0 %collective-permute-start.2 = (bf16[32,2304]{1,0:T(8,128)(2,1)S(1)}, bf16[32,2304]{1,0:T(8,128)(2,1)S(1)}, u32[]{:S(2)}, u32[]{:S(2)}) collective-permute-start(bf16[32,2304]{1,0:T(8,128)(2,1)S(1)} %get-tuple-element.23), channel_id=1, source_target_pairs={{0,64},{16,80},{32,96},{48,112},{64,0},{80,16},{96,32},{112,48},{1... | collective-permute-start | bytes 442376 | tf_op jit(solution)/shard_map/ppermute | solution.py:261
  99.1 10.2 %collective-permute-start.3 = (bf16[32,2304]{1,0:T(8,128)(2,1)S(1)}, bf16[32,2304]{1,0:T(8,128)(2,1)S(1)}, u32[]{:S(2)}, u32[]{:S(2)}) collective-permute-start(bf16[32,2304]{1,0:T(8,128)(2,1)S(1)} %get-tuple-element.24), channel_id=1, source_target_pairs={{0,80},{16,64},{32,112},{48,96},{64,16},{80,0},{96,48},{112,32},{1... | collective-permute-start | bytes 442376 | tf_op jit(solution)/shard_map/ppermute | solution.py:261
  101.7 11.4 %collective-permute-start.4 = (bf16[32,2304]{1,0:T(8,128)(2,1)S(1)}, bf16[32,2304]{1,0:T(8,128)(2,1)S(1)}, u32[]{:S(2)}, u32[]{:S(2)}) collective-permute-start(bf16[32,2304]{1,0:T(8,128)(2,1)S(1)} %get-tuple-element.25), channel_id=1, source_target_pairs={{0,32},{16,48},{32,64},{48,80},{64,96},{80,112},{96,0},{112,16},{1... | collective-permute-start | bytes 442376 | tf_op jit(solution)/shard_map/ppermute | solution.py:261
  102.6 10.5 %collective-permute-start.5 = (bf16[32,2304]{1,0:T(8,128)(2,1)S(1)}, bf16[32,2304]{1,0:T(8,128)(2,1)S(1)}, u32[]{:S(2)}, u32[]{:S(2)}) collective-permute-start(bf16[32,2304]{1,0:T(8,128)(2,1)S(1)} %get-tuple-element.26), channel_id=1, source_target_pairs={{0,96},{16,112},{32,0},{48,16},{64,32},{80,48},{96,64},{112,80},{1... | collective-permute-start | bytes 442376 | tf_op jit(solution)/shard_map/ppermute | solution.py:261
  105.5 7.7 %collective-permute-start.6 = (bf16[32,2304]{1,0:T(8,128)(2,1)S(1)}, bf16[32,2304]{1,0:T(8,128)(2,1)S(1)}, u32[]{:S(2)}, u32[]{:S(2)}) collective-permute-start(bf16[32,2304]{1,0:T(8,128)(2,1)S(1)} %get-tuple-element.27), channel_id=1, source_target_pairs={{0,16},{16,0},{32,48},{48,32},{64,80},{80,64},{96,112},{112,96},{1... | collective-permute-start | bytes 442376 | tf_op jit(solution)/shard_map/ppermute | solution.py:261
  109.3 6.5 %collective-permute-start = (bf16[32,2304]{1,0:T(8,128)(2,1)S(1)}, bf16[32,2304]{1,0:T(8,128)(2,1)S(1)}, u32[]{:S(2)}, u32[]{:S(2)}) collective-permute-start(bf16[32,2304]{1,0:T(8,128)(2,1)S(1)} %get-tuple-element.21), channel_id=1, source_target_pairs={{0,48},{16,32},{32,80},{48,64},{64,112},{80,96},{96,16},{112,0},{1... | collective-permute-start | bytes 442376 | tf_op jit(solution)/shard_map/ppermute | solution.py:261
  109.9 6.4 %collective-permute-start.1 = (bf16[32,2304]{1,0:T(8,128)(2,1)S(1)}, bf16[32,2304]{1,0:T(8,128)(2,1)S(1)}, u32[]{:S(2)}, u32[]{:S(2)}) collective-permute-start(bf16[32,2304]{1,0:T(8,128)(2,1)S(1)} %get-tuple-element.22), channel_id=1, source_target_pairs={{0,112},{16,96},{32,16},{48,0},{64,48},{80,32},{96,80},{112,64},{1... | collective-permute-start | bytes 442376 | tf_op jit(solution)/shard_map/ppermute | solution.py:261

commit v2 on v1

--- a/solution.py
+++ b/solution.py
@@ -14,7 +14,7 @@
 LATE = (4, 5)
 GROUP = 4
 AHEAD = 2
-HOPS = ((2, 0), (2, 1), (1, 0), (3, 0), (1, 1), (3, 1), (0, 1), (0, 0))
+HOPS = ((1, 0), (3, 0), (2, 0), (2, 1), (1, 1), (3, 1), (0, 1), (0, 0))
 
 
 def pack_kernel(chunks, owner_ref, counts_ref, field_ref, out_ref, buf, dst, pos_v, pos_s, sem_in, sem_pos, sem_out):
@@ -132,16 +132,12 @@
         for piece, row in zip(outs, places):
             piece[:, lanes] = out[pl.ds(pl.multiple_of(row * rows, rows), piece.shape[0]), lanes]
 
-    ahead = GROUP * AHEAD
     if staged:
         load.wait()
-        for q in range(ahead, ahead + GROUP):
-            fetch(q).start()
-        ahead += GROUP
     for g in range(0, count, GROUP):
         for q in range(max(g, staged), min(count, g + GROUP)):
             fetch(q).wait()
-        for q in range(g + ahead, min(count, g + ahead + GROUP)):
+        for q in range(g + GROUP * AHEAD, min(count, g + GROUP * AHEAD + GROUP)):
             fetch(q).start()
         if g:
             hand_out(g - GROUP)

time: 117 us -> 120 us (1.026)
  starting transfers between devices: 29.2 us -> 35.1 us
  waiting for transfers between devices: 63.5 us -> 59.9 us
    ppermute x11, starting transfers between devices: 17.2 us -> 23.2 us  [send(): return lax.ppermute(piece, 'el', pairs)]
    ppermute x11, waiting for transfers between devices: 14.2 us -> 10.5 us  [send(): return lax.ppermute(piece, 'el', pairs)]
  transfers between devices with their start and end apart: 12 -> 12, of which waited for: 8 -> 7; matrix products, arithmetic and copies ran while one was open for 0% -> 0% of each run, Pallas kernels for 9% -> 9%
where the time goes in v2:
time: 120 us; the launch traced here: 119 us
  waiting for transfers between devices  59.9 us (50%)
  starting transfers between devices  35.1 us (29%)
  Pallas kernels  24.1 us (20%)
    all_to_all x1, waiting for transfers between devices, on_device(): lax.all_to_all(outgoing, ('el', 'tg'), split_axis=0, concat_axis=0, tiled...  49.4 us
    ppermute x11, starting transfers between devices, send(): return lax.ppermute(piece, 'el', pairs)  23.2 us
    pallas_call x2, Pallas kernels, remap(): pl.pallas_call(functools.partial(remap_kernel, first, staged, paired, axi...  13.1 us
    all_to_all x1, starting transfers between devices, on_device(): lax.all_to_all(outgoing, ('el', 'tg'), split_axis=0, concat_axis=0, tiled...  12 us
    ppermute x11, waiting for transfers between devices, send(): return lax.ppermute(piece, 'el', pairs)  10.5 us
    pallas_call x1, Pallas kernels, pack(): pl.pallas_call(functools.partial(pack_kernel, chunks), out_shape=jax.Shap...  5.15 us
    pallas_call x3, Pallas kernels, join(): pl.pallas_call(functools.partial(join_kernel, start, groups, hops, axis),...  2.5 us
    pallas_call x1, Pallas kernels, stage(): pl.pallas_call(stage_kernel, out_shape=jax.ShapeDtypeStruct((STAGED, *wei...  2.46 us
  transfers between devices with their start and end apart: 12, of which 7 were waited for; matrix products, arithmetic and copies ran while one was open for 0% of the time, Pallas kernels for 9%

profile of v2, /device:TPU:1, one launch (start us, length us, event | category | flops | bytes accessed | tf_op | source)
XLA Modules:
  0.0 119.3 jit_solution(18287347111381814334)
XLA Ops:
  0.0 5.1 %pack.1 = bf16[512,16,256]{2,1,0:T(8,128)(2,1)} custom-call(s32[1,512]{1,0:T(1,128)} %owner_ref.1, s32[1,512]{1,0:T(1,128)} %counts_ref.1, bf16[512,16,256]{2,1,0:T(8,128)(2,1)} %field_ref.1), custom_call_target="tpu_custom_call" | custom-call | tf_op jit(solution)/shard_map/pack/pallas_call | solution.py:56
  5.2 12.0 %all-to-all-start = ((bf16[128,64,256]{2,1,0:T(8,128)(2,1)}), bf16[128,64,256]{2,1,0:T(8,128)(2,1)}, u32[]{:S(2)}, u32[]{:S(2)}) async-start(bf16[128,64,256]{2,1,0:T(8,128)(2,1)} %bitcast.2), calls=%async_computation | async-start | bytes 8388608 | tf_op jit(solution)/shard_map/all_to_all | solution.py:266
  17.2 2.5 %stage.1.refs_0_ = bf16[6,16,128,128]{3,2,1,0:T(8,128)(2,1)S(1)} custom-call(s32[1,32]{1,0:T(1,128)S(1)} %copy-done, bf16[1,32,16,128,128]{4,3,2,1,0:T(8,128)(2,1)} %w_ref.5), custom_call_target="tpu_custom_call" | custom-call | bytes 6291456 | tf_op jit(solution)/shard_map/stage/pallas_call | solution.py:93
  19.7 49.4 %all-to-all-done = bf16[128,64,256]{2,1,0:T(8,128)(2,1)} async-done(((bf16[128,64,256]{2,1,0:T(8,128)(2,1)}), bf16[128,64,256]{2,1,0:T(8,128)(2,1)}, u32[]{:S(2)}, u32[]{:S(2)}) %all-to-all-start) | async-done | bytes 4194336 | tf_op jit(solution)/shard_map/all_to_all | solution.py:266
  69.1 6.6 %shard_map.64 = (bf16[64,1792]{1,0:T(8,128)(2,1)S(1)}, bf16[64,1792]{1,0:T(8,128)(2,1)S(1)}, bf16[64,1792]{1,0:T(8,128)(2,1)S(1)}, bf16[64,1792]{1,0:T(8,128)(2,1)S(1)}, bf16[64,128,256]{2,1,0:T(8,128)(2,1)S(1)}) custom-call(s32[1,32]{1,0:T(1,128)S(1)} %copy-done, s32[1,32,16]{2,1,0:T(8,128)S(1)} %copy.11.cols_ref, bf16[1,32,16,128,128]{4,3,2,1,0:T(8,128)(2,1)} %w_ref.5, ...), custom_call_target="tpu_custom_call" | custom-call | flops 1879048192 | bytes 11534336 | tf_op jit(solution)/shard_map/pallas_call | solution.py:166
  75.8 2.7 %collective-permute-start.8 = (bf16[64,1792]{1,0:T(8,128)(2,1)S(1)}, bf16[64,1792]{1,0:T(8,128)(2,1)S(1)}, u32[]{:S(2)}, u32[]{:S(2)}) collective-permute-start(bf16[64,1792]{1,0:T(8,128)(2,1)S(1)} %get-tuple-element.30), channel_id=1, source_target_pairs={{0,96},{16,112},{32,0},{48,16},{64,32},{80,48},{96,64},{112,80},{1... | collective-permute-start | bytes 688136 | tf_op jit(solution)/shard_map/ppermute | solution.py:257
  78.5 1.6 %collective-permute-start.9 = (bf16[64,1792]{1,0:T(8,128)(2,1)S(1)}, bf16[64,1792]{1,0:T(8,128)(2,1)S(1)}, u32[]{:S(2)}, u32[]{:S(2)}) collective-permute-start(bf16[64,1792]{1,0:T(8,128)(2,1)S(1)} %get-tuple-element.31), channel_id=1, source_target_pairs={{0,64},{16,80},{32,96},{48,112},{64,0},{80,16},{96,32},{112,48},{1... | collective-permute-start | bytes 688136 | tf_op jit(solution)/shard_map/ppermute | solution.py:257
  80.2 2.6 %collective-permute-done.7.refs_0_ = bf16[64,1792]{1,0:T(8,128)(2,1)S(1)} collective-permute-done((bf16[64,1792]{1,0:T(8,128)(2,1)S(1)}, bf16[64,1792]{1,0:T(8,128)(2,1)S(1)}, u32[]{:S(2)}, u32[]{:S(2)}) %collective-permute-start.7) | collective-permute-done | bytes 229408 | tf_op jit(solution)/shard_map/ppermute | solution.py:257
  82.7 0.5 collective-permute-done.8.refs_1_
  83.2 5.5 %collective-permute-done.9.refs_2_ = bf16[64,1792]{1,0:T(8,128)(2,1)S(1)} collective-permute-done((bf16[64,1792]{1,0:T(8,128)(2,1)S(1)}, bf16[64,1792]{1,0:T(8,128)(2,1)S(1)}, u32[]{:S(2)}, u32[]{:S(2)}) %collective-permute-start.9) | collective-permute-done | bytes 229408 | tf_op jit(solution)/shard_map/ppermute | solution.py:257
  88.7 0.8 shard_map.66
  89.5 2.5 %collective-permute-start.10 = (bf16[128,1792]{1,0:T(8,128)(2,1)S(1)}, bf16[128,1792]{1,0:T(8,128)(2,1)S(1)}, u32[]{:S(2)}, u32[]{:S(2)}) collective-permute-start(bf16[128,1792]{1,0:T(8,128)(2,1)S(1)} %get-tuple-element.33), channel_id=1, source_target_pairs={{0,16},{16,0},{32,48},{48,32},{64,80},{80,64},{96,112},{112,96},{1... | collective-permute-start | bytes 1376264 | tf_op jit(solution)/shard_map/ppermute | solution.py:257
  92.0 6.5 %shard_map.65 = (bf16[32,2304]{1,0:T(8,128)(2,1)S(1)}, bf16[32,2304]{1,0:T(8,128)(2,1)S(1)}, bf16[32,2304]{1,0:T(8,128)(2,1)S(1)}, bf16[32,2304]{1,0:T(8,128)(2,...) custom-call(s32[1,32]{1,0:T(1,128)S(1)} %copy-done, ...), custom_call_target="tpu_custom_call" | custom-call | flops 2415919104 | bytes 13631488 | tf_op jit(solution)/shard_map/pallas_call | solution.py:166
  98.5 0.9 collective-permute-start.2
  99.5 1.8 %collective-permute-start.3 = (bf16[32,2304]{1,0:T(8,128)(2,1)S(1)}, bf16[32,2304]{1,0:T(8,128)(2,1)S(1)}, u32[]{:S(2)}, u32[]{:S(2)}) collective-permute-start(bf16[32,2304]{1,0:T(8,128)(2,1)S(1)} %get-tuple-element.24), channel_id=1, source_target_pairs={{0,96},{16,112},{32,0},{48,16},{64,32},{80,48},{96,64},{112,80},{1... | collective-permute-start | bytes 442376 | tf_op jit(solution)/shard_map/ppermute | solution.py:257
  101.4 3.6 %collective-permute-start.5 = (bf16[32,2304]{1,0:T(8,128)(2,1)S(1)}, bf16[32,2304]{1,0:T(8,128)(2,1)S(1)}, u32[]{:S(2)}, u32[]{:S(2)}) collective-permute-start(bf16[32,2304]{1,0:T(8,128)(2,1)S(1)} %get-tuple-element.26), channel_id=1, source_target_pairs={{0,80},{16,64},{32,112},{48,96},{64,16},{80,0},{96,48},{112,32},{1... | collective-permute-start | bytes 442376 | tf_op jit(solution)/shard_map/ppermute | solution.py:257
  105.0 0.2 collective-permute-done.2.refs_0_
  105.2 1.1 collective-permute-start.6
  106.3 8.7 %collective-permute-start.1 = (bf16[32,2304]{1,0:T(8,128)(2,1)S(1)}, bf16[32,2304]{1,0:T(8,128)(2,1)S(1)}, u32[]{:S(2)}, u32[]{:S(2)}) collective-permute-start(bf16[32,2304]{1,0:T(8,128)(2,1)S(1)} %get-tuple-element.22), channel_id=1, source_target_pairs={{0,112},{16,96},{32,16},{48,0},{64,48},{80,32},{96,80},{112,64},{1... | collective-permute-start | bytes 442376 | tf_op jit(solution)/shard_map/ppermute | solution.py:257
  115.0 0.8 shard_map.67.refs_6_
  115.8 1.0 shard_map.68.refs_2_
  116.8 1.6 %collective-permute-done.refs_0_ = bf16[32,2304]{1,0:T(8,128)(2,1)S(1)} collective-permute-done((bf16[32,2304]{1,0:T(8,128)(2,1)S(1)}, bf16[32,2304]{1,0:T(8,128)(2,1)S(1)}, u32[]{:S(2)}, u32[]{:S(2)}) %collective-permute-start) | collective-permute-done | bytes 147488 | tf_op jit(solution)/shard_map/ppermute | solution.py:257
  118.4 0.2 collective-permute-done.1.refs_1_
  118.6 0.7 shard_map.69
  (13 shorter events, 0.3 us)
Async XLA Ops:
  5.2 12.0 %copy-start.1 = (s32[1,32,16]{1,2,0:T(8,128)S(1)}, s32[1,32,16]{1,2,0:T(8,128)}, u32[]{:S(2)}) copy-start(s32[1,32,16]{1,2,0:T(8,128)} %param.10) | copy-start | bytes 6148
  5.2 12.1 %copy-start = (s32[1,32]{1,0:T(1,128)S(1)}, s32[1,32]{1,0:T(1,128)}, u32[]{:S(2)}) copy-start(s32[1,32]{1,0:T(1,128)} %rows_ref.5) | copy-start | bytes 388
  5.2 63.9 %all-to-all-start = ((bf16[128,64,256]{2,1,0:T(8,128)(2,1)}), bf16[128,64,256]{2,1,0:T(8,128)(2,1)}, u32[]{:S(2)}, u32[]{:S(2)}) async-start(bf16[128,64,256]{2,1,0:T(8,128)(2,1)} %bitcast.2), calls=%async_computation | async-start | bytes 8388608 | tf_op jit(solution)/shard_map/all_to_all | solution.py:266
  75.7 7.0 %collective-permute-start.7 = (bf16[64,1792]{1,0:T(8,128)(2,1)S(1)}, bf16[64,1792]{1,0:T(8,128)(2,1)S(1)}, u32[]{:S(2)}, u32[]{:S(2)}) collective-permute-start(bf16[64,1792]{1,0:T(8,128)(2,1)S(1)} %get-tuple-element.29), channel_id=1, source_target_pairs={{0,32},{16,48},{32,64},{48,80},{64,96},{80,112},{96,0},{112,16},{1... | collective-permute-start | bytes 688136 | tf_op jit(solution)/shard_map/ppermute | solution.py:257
  75.8 7.4 %collective-permute-start.8 = (bf16[64,1792]{1,0:T(8,128)(2,1)S(1)}, bf16[64,1792]{1,0:T(8,128)(2,1)S(1)}, u32[]{:S(2)}, u32[]{:S(2)}) collective-permute-start(bf16[64,1792]{1,0:T(8,128)(2,1)S(1)} %get-tuple-element.30), channel_id=1, source_target_pairs={{0,96},{16,112},{32,0},{48,16},{64,32},{80,48},{96,64},{112,80},{1... | collective-permute-start | bytes 688136 | tf_op jit(solution)/shard_map/ppermute | solution.py:257
  78.5 10.1 %collective-permute-start.9 = (bf16[64,1792]{1,0:T(8,128)(2,1)S(1)}, bf16[64,1792]{1,0:T(8,128)(2,1)S(1)}, u32[]{:S(2)}, u32[]{:S(2)}) collective-permute-start(bf16[64,1792]{1,0:T(8,128)(2,1)S(1)} %get-tuple-element.31), channel_id=1, source_target_pairs={{0,64},{16,80},{32,96},{48,112},{64,0},{80,16},{96,32},{112,48},{1... | collective-permute-start | bytes 688136 | tf_op jit(solution)/shard_map/ppermute | solution.py:257
  89.5 16.8 %collective-permute-start.10 = (bf16[128,1792]{1,0:T(8,128)(2,1)S(1)}, bf16[128,1792]{1,0:T(8,128)(2,1)S(1)}, u32[]{:S(2)}, u32[]{:S(2)}) collective-permute-start(bf16[128,1792]{1,0:T(8,128)(2,1)S(1)} %get-tuple-element.33), channel_id=1, source_target_pairs={{0,16},{16,0},{32,48},{48,32},{64,80},{80,64},{96,112},{112,96},{1... | collective-permute-start | bytes 1376264 | tf_op jit(solution)/shard_map/ppermute | solution.py:257
  98.5 6.7 %collective-permute-start.2 = (bf16[32,2304]{1,0:T(8,128)(2,1)S(1)}, bf16[32,2304]{1,0:T(8,128)(2,1)S(1)}, u32[]{:S(2)}, u32[]{:S(2)}) collective-permute-start(bf16[32,2304]{1,0:T(8,128)(2,1)S(1)} %get-tuple-element.23), channel_id=1, source_target_pairs={{0,32},{16,48},{32,64},{48,80},{64,96},{80,112},{96,0},{112,16},{1... | collective-permute-start | bytes 442376 | tf_op jit(solution)/shard_map/ppermute | solution.py:257
  99.5 6.8 %collective-permute-start.3 = (bf16[32,2304]{1,0:T(8,128)(2,1)S(1)}, bf16[32,2304]{1,0:T(8,128)(2,1)S(1)}, u32[]{:S(2)}, u32[]{:S(2)}) collective-permute-start(bf16[32,2304]{1,0:T(8,128)(2,1)S(1)} %get-tuple-element.24), channel_id=1, source_target_pairs={{0,96},{16,112},{32,0},{48,16},{64,32},{80,48},{96,64},{112,80},{1... | collective-permute-start | bytes 442376 | tf_op jit(solution)/shard_map/ppermute | solution.py:257
  101.3 14.5 %collective-permute-start.4 = (bf16[32,2304]{1,0:T(8,128)(2,1)S(1)}, bf16[32,2304]{1,0:T(8,128)(2,1)S(1)}, u32[]{:S(2)}, u32[]{:S(2)}) collective-permute-start(bf16[32,2304]{1,0:T(8,128)(2,1)S(1)} %get-tuple-element.25), channel_id=1, source_target_pairs={{0,64},{16,80},{32,96},{48,112},{64,0},{80,16},{96,32},{112,48},{1... | collective-permute-start | bytes 442376 | tf_op jit(solution)/shard_map/ppermute | solution.py:257
  101.4 14.4 %collective-permute-start.5 = (bf16[32,2304]{1,0:T(8,128)(2,1)S(1)}, bf16[32,2304]{1,0:T(8,128)(2,1)S(1)}, u32[]{:S(2)}, u32[]{:S(2)}) collective-permute-start(bf16[32,2304]{1,0:T(8,128)(2,1)S(1)} %get-tuple-element.26), channel_id=1, source_target_pairs={{0,80},{16,64},{32,112},{48,96},{64,16},{80,0},{96,48},{112,32},{1... | collective-permute-start | bytes 442376 | tf_op jit(solution)/shard_map/ppermute | solution.py:257
  105.2 10.6 %collective-permute-start.6 = (bf16[32,2304]{1,0:T(8,128)(2,1)S(1)}, bf16[32,2304]{1,0:T(8,128)(2,1)S(1)}, u32[]{:S(2)}, u32[]{:S(2)}) collective-permute-start(bf16[32,2304]{1,0:T(8,128)(2,1)S(1)} %get-tuple-element.27), channel_id=1, source_target_pairs={{0,16},{16,0},{32,48},{48,32},{64,80},{80,64},{96,112},{112,96},{1... | collective-permute-start | bytes 442376 | tf_op jit(solution)/shard_map/ppermute | solution.py:257
  106.2 12.1 %collective-permute-start = (bf16[32,2304]{1,0:T(8,128)(2,1)S(1)}, bf16[32,2304]{1,0:T(8,128)(2,1)S(1)}, u32[]{:S(2)}, u32[]{:S(2)}) collective-permute-start(bf16[32,2304]{1,0:T(8,128)(2,1)S(1)} %get-tuple-element.21), channel_id=1, source_target_pairs={{0,48},{16,32},{32,80},{48,64},{64,112},{80,96},{96,16},{112,0},{1... | collective-permute-start | bytes 442376 | tf_op jit(solution)/shard_map/ppermute | solution.py:257
  106.3 12.3 %collective-permute-start.1 = (bf16[32,2304]{1,0:T(8,128)(2,1)S(1)}, bf16[32,2304]{1,0:T(8,128)(2,1)S(1)}, u32[]{:S(2)}, u32[]{:S(2)}) collective-permute-start(bf16[32,2304]{1,0:T(8,128)(2,1)S(1)} %get-tuple-element.22), channel_id=1, source_target_pairs={{0,112},{16,96},{32,16},{48,0},{64,48},{80,32},{96,80},{112,64},{1... | collective-permute-start | bytes 442376 | tf_op jit(solution)/shard_map/ppermute | solution.py:257
